TPU v7x, 32 devices: a whole 2x2x4 slice. The times are simulated.
32 devices in a mesh: grp: 2 (over y), cell: 4 (over z), snap: 2 (over x), var: 2 (over core).
Axes of the slice: x: 2, y: 2, z: 4, core: 2. Of those that a mesh axis runs over, the one named last changes fastest.
Arguments:
- q_true: bfloat16 [64, 10, 2048], P(('snap', 'var'), 'grp', 'cell'), parts along dimension 1, may hold values from -6 to 6
- coeffs: bfloat16 [64, 256], P(('snap', 'var'), 'grp'), parts along dimension 1, may hold values from -0.5 to 0.5
- basis: bfloat16 [128, 10, 2048], P(('snap', 'var'), 'grp', 'cell'), parts along dimension 1, may hold values from -6 to 6
- weights: float32 [10, 2048], P('grp', 'cell'), parts along dimension 0, may hold values from 0.0029646354 to 0.029646354
- geometry: float32 [12, 2048], P('grp', 'cell'), parts along dimension 0, may hold values from 0.2 to 1
- neighbors: int32 [12, 2048], P('grp', 'cell'), parts along dimension 0, may hold values from 0 to 767, as said below
- send_rows: int32 [4, 4, 128], P('cell', 'grp'), parts along dimension 1, may hold values from 0 to 511, as said below
- block_count: int32 [4, 2], P('cell', 'grp'), parts along dimension 1, may hold values from 2 to 4
Outputs:
- closure: float32 [64, 256], P(('snap', 'var'), 'grp'), parts along dimension 1
There are 2 independent parts, one for each index of `grp`. A program takes and returns all parts, laid end to end along the dimension named above; each array names one. Nothing has to cross between parts.
Inputs may be any that keep to these rules, and one draw needn't show every extreme that they name: neighbors[k, c] indexes a list made of the 512 cells of c's own cell shard, then the 128 cells received from the shard before, then the 128 cells received from the shard after. `send_rows`: indices local to the sending cell shard.
All inputs are finite; a program needn't handle non-finite values.
Results may differ from a plain program's by a relative error of at most 0.00091.
Values may be sent and summed in bfloat16 or wider, within the bound.
A program may use at most 64 MiB of HBM per device.

v0:
```python
import math
import jax
import jax.numpy as jnp
from jax import lax
from jax.sharding import PartitionSpec as P

BLOCK = 128


def from_behind(shard, axis, by):
    peers = lax.axis_size(axis)
    pairs = [(i, i + by) for i in range(peers) if 0 <= i + by < peers]
    return lax.ppermute(shard, axis, pairs)


def face_flux(extended, geometry, neighbors):
    cell_count = geometry.shape[1]
    var_count = extended.shape[1]
    own_cells = extended[:, :, :cell_count]
    product = extended * extended[:, 1:2, :]
    own_product = product[:, :, :cell_count]
    stacked = jnp.concatenate([extended, product], axis=1)
    running = jnp.zeros(own_cells.shape, jnp.float32)
    for face_index in range(geometry.shape[0]):
        taken = jnp.take(stacked, neighbors[face_index], axis=2)
        beside = taken[:, :var_count]
        beside_product = taken[:, var_count:]
        running = running + geometry[face_index] * (
            0.5 * (own_product + beside_product) - 0.5 * (beside - own_cells)
        )
    return running


def local(q_true, coeffs, basis, weights, geometry, neighbors, send_rows, block_count):
    snap_count, var_count, cell_count = q_true.shape
    send_lists = send_rows[0]

    def rim_rows(field):
        return (jnp.take(field, send_lists[0], axis=2), jnp.take(field, send_lists[1], axis=2))

    true_to_prev, true_to_next = rim_rows(q_true)
    whole_basis = lax.all_gather(basis, ("snap", "var"), axis=0, tiled=True)
    basis_flat = whole_basis.reshape(whole_basis.shape[0], var_count * cell_count)
    rebuilt_sum = jnp.dot(coeffs, basis_flat, preferred_element_type=jnp.float32)
    rebuilt = rebuilt_sum.astype(jnp.bfloat16).reshape(snap_count, var_count, cell_count)
    rebuilt_to_prev, rebuilt_to_next = rim_rows(rebuilt)
    true_from_prev = from_behind(true_to_next, "cell", 1)
    true_from_next = from_behind(true_to_prev, "cell", -1)
    rebuilt_from_prev = from_behind(rebuilt_to_next, "cell", 1)
    rebuilt_from_next = from_behind(rebuilt_to_prev, "cell", -1)
    true_ext = jnp.concatenate([q_true, true_from_prev, true_from_next], axis=2)
    rebuilt_ext = jnp.concatenate([rebuilt, rebuilt_from_prev, rebuilt_from_next], axis=2)
    positions = jnp.arange(cell_count, dtype=jnp.int32)
    live = (positions < block_count[0, 0] * BLOCK).astype(jnp.float32)
    group = math.gcd(snap_count, 8)
    ext_count = true_ext.shape[2]

    def snap_block(pair):
        true_part, rebuilt_part = pair
        flux_true = face_flux(true_part.astype(jnp.float32), geometry, neighbors)
        flux_rebuilt = face_flux(rebuilt_part.astype(jnp.float32), geometry, neighbors)
        return (weights * live * (flux_true - flux_rebuilt)).astype(jnp.bfloat16)

    true_groups = true_ext.reshape(snap_count // group, group, var_count, ext_count)
    rebuilt_groups = rebuilt_ext.reshape(snap_count // group, group, var_count, ext_count)
    weighted = lax.map(snap_block, (true_groups, rebuilt_groups))
    weighted_flat = weighted.reshape(snap_count, var_count * cell_count)
    contract = (((1,), (1,)), ((), ()))
    closure_part = lax.dot_general(
        weighted_flat, basis_flat, contract, preferred_element_type=jnp.float32
    )
    return lax.psum(closure_part, "cell")


def solution(mesh):
    in_specs = (
        P(("snap", "var"), "grp", "cell"),
        P(("snap", "var"), "grp"),
        P(("snap", "var"), "grp", "cell"),
        P("grp", "cell"),
        P("grp", "cell"),
        P("grp", "cell"),
        P("cell", "grp", None),
        P("cell", "grp"),
    )
    out_specs = P(("snap", "var"), "grp")
    return jax.shard_map(local, mesh=mesh, in_specs=in_specs, out_specs=out_specs, check_vma=False)
```

profile of v0, /device:TPU:0, one launch (start us, length us, event | category | flops | bytes accessed | tf_op | source)
XLA Modules:
  0.0 230.5 jit_solution(12883758674813576312)
XLA Ops:
  0.8 9.7 %all_gather.3 = bf16[128,5,512]{2,0,1:T(8,128)(2,1)S(1)} all-gather(bf16[32,5,512]{2,0,1:T(8,128)(2,1)} %param.16), channel_id=1, replica_groups=mesh['grp'=2,'cell'=4,'snap'=2,'var'=2] {'snap','var'}, dimensions={0}, use_global_device_ids=true | all-gather | bytes 819200 | tf_op jit(solution)/shard_map/all_gather | solution.py:42
  15.2 3.5 %collective-permute-start = (bf16[16,5,128]{0,1,2:T(8,128)(2,1)}, bf16[16,5,128]{0,1,2:T(8,128)(2,1)S(1)}, u32[]{:S(2)}, u32[]{:S(2)}) collective-permute-start(bf16[16,5,128]{0,1,2:T(8,128)(2,1)} %get-tuple-element.158), channel_id=1, source_target_pairs={{0,4},{4,8},{8,12},{1,5},{5,9},{9,13},{2,6},{6,10},{10,14},{3,7},{... | collective-permute-start | bytes 61448 | tf_op jit(solution)/shard_map/ppermute | solution.py:13
  21.6 4.6 %collective-permute-start.2 = (bf16[16,5,128]{0,1,2:T(8,128)(2,1)}, bf16[16,5,128]{0,1,2:T(8,128)(2,1)S(1)}, u32[]{:S(2)}, u32[]{:S(2)}) collective-permute-start(bf16[16,5,128]{0,1,2:T(8,128)(2,1)} %get-tuple-element.157), channel_id=1, source_target_pairs={{0,4},{4,8},{8,12},{1,5},{5,9},{9,13},{2,6},{6,10},{10,14},{3,7},{... | collective-permute-start | bytes 61448 | tf_op jit(solution)/shard_map/ppermute | solution.py:13
  32.1 4.0 %collective-permute-done.3 = bf16[16,5,128]{0,1,2:T(8,128)(2,1)S(1)} collective-permute-done((bf16[16,5,128]{0,1,2:T(8,128)(2,1)S(1)}, bf16[16,5,128]{0,1,2:T(8,128)(2,1)S(1)}, u32[]{:S(2)}, u32[]{:S(2)}) %collective-permute-start.3) | collective-permute-done | bytes 20512 | tf_op jit(solution)/shard_map/ppermute | solution.py:13
  36.9 181.6 %while.11 = (s32[]{:T(128)}, bf16[2,8,5,512]{3,1,2,0:T(8,128)(2,1)}, f32[5,512]{1,0:T(8,128)S(1)}, f32[6,512]{1,0:T(8,128)}, bf16[2,8,5,768]{3,1,0,2:T(8,128)(2,...) while((s32[]{:T(128)}, ...), condition=%wide.region_1.4_spmd.clone, body=%wide.region_0.3_spmd.clone.sunk | while | flops 2576898 | bytes 26133308 | solution.py:66
  49.7 2.8 %gather_fusion.11 = f32[512,8,10]{2,1,0:T(8,128)} fusion(f32[8,10,768]{1,0,2:T(8,128)S(1)} %copy.153, s32[1024]{0:T(1024)} %pad_clamp_fusion.19), kind=kCustom, calls=%fused_computation.10.clone.clone.1 | custom fusion | bytes 329728 | tf_op jit(solution)/shard_map/while/body/eval_jaxpr/jit(_take)/gather | solution.py:25
  52.5 2.9 %copy.164 = f32[512,8,10]{0,1,2:T(8,128)} copy(f32[512,8,10]{2,1,0:T(8,128)} %gather_fusion.11) | data formatting | bytes 327680 | tf_op jit(solution)/shard_map/while/body/eval_jaxpr/jit(_take)/gather | solution.py:25
  58.1 2.9 %copy.162 = f32[512,8,10]{0,1,2:T(8,128)} copy(f32[512,8,10]{2,1,0:T(8,128)} %gather_fusion.9) | data formatting | bytes 327680 | tf_op jit(solution)/shard_map/while/body/eval_jaxpr/jit(_take)/gather | solution.py:25
  63.6 2.9 %copy.160 = f32[512,8,10]{0,1,2:T(8,128)} copy(f32[512,8,10]{2,1,0:T(8,128)} %gather_fusion.7) | data formatting | bytes 327680 | tf_op jit(solution)/shard_map/while/body/eval_jaxpr/jit(_take)/gather | solution.py:25
  69.2 2.9 %copy.158 = f32[512,8,10]{0,1,2:T(8,128)} copy(f32[512,8,10]{2,1,0:T(8,128)} %gather_fusion.5) | data formatting | bytes 327680 | tf_op jit(solution)/shard_map/while/body/eval_jaxpr/jit(_take)/gather | solution.py:25
  74.8 2.9 %copy.156 = f32[512,8,10]{0,1,2:T(8,128)} copy(f32[512,8,10]{2,1,0:T(8,128)} %gather_fusion.3) | data formatting | bytes 327680 | tf_op jit(solution)/shard_map/while/body/eval_jaxpr/jit(_take)/gather | solution.py:25
  80.3 2.9 %copy.154 = f32[512,8,10]{0,1,2:T(8,128)} copy(f32[512,8,10]{2,1,0:T(8,128)} %gather_fusion.1) | data formatting | bytes 327680 | tf_op jit(solution)/shard_map/while/body/eval_jaxpr/jit(_take)/gather | solution.py:25
  85.4 2.8 %gather_fusion.10 = f32[512,8,10]{2,1,0:T(8,128)} fusion(f32[8,10,768]{1,0,2:T(8,128)S(1)} %copy.151, s32[1024]{0:T(1024)} %pad_clamp_fusion.19), kind=kCustom, calls=%fused_computation.1.clone.clone.1 | custom fusion | bytes 329728 | tf_op jit(solution)/shard_map/while/body/eval_jaxpr/jit(_take)/gather | solution.py:25
  88.2 2.9 %copy.163 = f32[512,8,10]{0,1,2:T(8,128)} copy(f32[512,8,10]{2,1,0:T(8,128)} %gather_fusion.10) | data formatting | bytes 327680 | tf_op jit(solution)/shard_map/while/body/eval_jaxpr/jit(_take)/gather | solution.py:25
  95.5 2.9 %copy.161 = f32[512,8,10]{0,1,2:T(8,128)} copy(f32[512,8,10]{2,1,0:T(8,128)} %gather_fusion.8) | data formatting | bytes 327680 | tf_op jit(solution)/shard_map/while/body/eval_jaxpr/jit(_take)/gather | solution.py:25
  102.9 2.9 %copy.159 = f32[512,8,10]{0,1,2:T(8,128)} copy(f32[512,8,10]{2,1,0:T(8,128)} %gather_fusion.6) | data formatting | bytes 327680 | tf_op jit(solution)/shard_map/while/body/eval_jaxpr/jit(_take)/gather | solution.py:25
  110.3 2.9 %copy.157 = f32[512,8,10]{0,1,2:T(8,128)} copy(f32[512,8,10]{2,1,0:T(8,128)} %gather_fusion.4) | data formatting | bytes 327680 | tf_op jit(solution)/shard_map/while/body/eval_jaxpr/jit(_take)/gather | solution.py:25
  117.6 2.9 %copy.155 = f32[512,8,10]{0,1,2:T(8,128)} copy(f32[512,8,10]{2,1,0:T(8,128)} %gather_fusion.2) | data formatting | bytes 327680 | tf_op jit(solution)/shard_map/while/body/eval_jaxpr/jit(_take)/gather | solution.py:25
  140.5 2.8 %gather_fusion.11 = f32[512,8,10]{2,1,0:T(8,128)} fusion(f32[8,10,768]{1,0,2:T(8,128)S(1)} %copy.153, s32[1024]{0:T(1024)} %pad_clamp_fusion.19), kind=kCustom, calls=%fused_computation.10.clone.clone.1 | custom fusion | bytes 329728 | tf_op jit(solution)/shard_map/while/body/eval_jaxpr/jit(_take)/gather | solution.py:25
  143.3 2.9 %copy.164 = f32[512,8,10]{0,1,2:T(8,128)} copy(f32[512,8,10]{2,1,0:T(8,128)} %gather_fusion.11) | data formatting | bytes 327680 | tf_op jit(solution)/shard_map/while/body/eval_jaxpr/jit(_take)/gather | solution.py:25
  148.9 2.9 %copy.162 = f32[512,8,10]{0,1,2:T(8,128)} copy(f32[512,8,10]{2,1,0:T(8,128)} %gather_fusion.9) | data formatting | bytes 327680 | tf_op jit(solution)/shard_map/while/body/eval_jaxpr/jit(_take)/gather | solution.py:25
  154.4 2.9 %copy.160 = f32[512,8,10]{0,1,2:T(8,128)} copy(f32[512,8,10]{2,1,0:T(8,128)} %gather_fusion.7) | data formatting | bytes 327680 | tf_op jit(solution)/shard_map/while/body/eval_jaxpr/jit(_take)/gather | solution.py:25
  160.0 2.9 %copy.158 = f32[512,8,10]{0,1,2:T(8,128)} copy(f32[512,8,10]{2,1,0:T(8,128)} %gather_fusion.5) | data formatting | bytes 327680 | tf_op jit(solution)/shard_map/while/body/eval_jaxpr/jit(_take)/gather | solution.py:25
  165.6 2.9 %copy.156 = f32[512,8,10]{0,1,2:T(8,128)} copy(f32[512,8,10]{2,1,0:T(8,128)} %gather_fusion.3) | data formatting | bytes 327680 | tf_op jit(solution)/shard_map/while/body/eval_jaxpr/jit(_take)/gather | solution.py:25
  171.1 2.9 %copy.154 = f32[512,8,10]{0,1,2:T(8,128)} copy(f32[512,8,10]{2,1,0:T(8,128)} %gather_fusion.1) | data formatting | bytes 327680 | tf_op jit(solution)/shard_map/while/body/eval_jaxpr/jit(_take)/gather | solution.py:25
  176.2 2.8 %gather_fusion.10 = f32[512,8,10]{2,1,0:T(8,128)} fusion(f32[8,10,768]{1,0,2:T(8,128)S(1)} %copy.151, s32[1024]{0:T(1024)} %pad_clamp_fusion.19), kind=kCustom, calls=%fused_computation.1.clone.clone.1 | custom fusion | bytes 329728 | tf_op jit(solution)/shard_map/while/body/eval_jaxpr/jit(_take)/gather | solution.py:25
  179.0 2.9 %copy.163 = f32[512,8,10]{0,1,2:T(8,128)} copy(f32[512,8,10]{2,1,0:T(8,128)} %gather_fusion.10) | data formatting | bytes 327680 | tf_op jit(solution)/shard_map/while/body/eval_jaxpr/jit(_take)/gather | solution.py:25
  186.3 2.9 %copy.161 = f32[512,8,10]{0,1,2:T(8,128)} copy(f32[512,8,10]{2,1,0:T(8,128)} %gather_fusion.8) | data formatting | bytes 327680 | tf_op jit(solution)/shard_map/while/body/eval_jaxpr/jit(_take)/gather | solution.py:25
  193.7 2.9 %copy.159 = f32[512,8,10]{0,1,2:T(8,128)} copy(f32[512,8,10]{2,1,0:T(8,128)} %gather_fusion.6) | data formatting | bytes 327680 | tf_op jit(solution)/shard_map/while/body/eval_jaxpr/jit(_take)/gather | solution.py:25
  201.1 2.9 %copy.157 = f32[512,8,10]{0,1,2:T(8,128)} copy(f32[512,8,10]{2,1,0:T(8,128)} %gather_fusion.4) | data formatting | bytes 327680 | tf_op jit(solution)/shard_map/while/body/eval_jaxpr/jit(_take)/gather | solution.py:25
  208.4 2.9 %copy.155 = f32[512,8,10]{0,1,2:T(8,128)} copy(f32[512,8,10]{2,1,0:T(8,128)} %gather_fusion.2) | data formatting | bytes 327680 | tf_op jit(solution)/shard_map/while/body/eval_jaxpr/jit(_take)/gather | solution.py:25
  219.8 10.7 %psum.7 = f32[16,128]{1,0:T(8,128)} all-reduce(f32[16,128]{1,0:T(8,128)S(1)} %fusion.66), channel_id=1, replica_groups=mesh['grp'=2,'cell'=4,'snap'=2,'var'=2] {'cell'}, use_global_device_ids=true, to_apply=%region_2.5 | all-reduce | flops 2048 | bytes 16384 | tf_op jit(solution)/shard_map/psum | solution.py:72
  (233 shorter events, 121.8 us)
Async XLA Ops:
  0.0 10.8 %copy-start = (bf16[16,128]{1,0:T(8,128)(2,1)S(1)}, bf16[16,128]{1,0:T(8,128)(2,1)}, u32[]{:S(2)}) copy-start(bf16[16,128]{1,0:T(8,128)(2,1)} %param.15) | copy-start | bytes 12292
  0.8 11.3 %copy-start.17 = (bf16[16,5,512]{2,0,1:T(8,128)(2,1)S(1)}, bf16[16,5,512]{2,0,1:T(8,128)(2,1)}, u32[]{:S(2)}) copy-start(bf16[16,5,512]{2,0,1:T(8,128)(2,1)} %param.14) | copy-start | bytes 245764
  10.8 4.4 %copy-start.14 = (bf16[128,5,512]{0,2,1:T(8,128)(2,1)}, bf16[128,5,512]{0,2,1:T(8,128)(2,1)S(1)}, u32[]{:S(2)}) copy-start(bf16[128,5,512]{0,2,1:T(8,128)(2,1)S(1)} %copy.124) | copy-start | bytes 1966084
  12.8 24.1 %copy-start.15 = (f32[5,512]{1,0:T(8,128)S(1)}, f32[5,512]{1,0:T(8,128)}, u32[]{:S(2)}) copy-start(f32[5,512]{1,0:T(8,128)} %param.17) | copy-start | bytes 30724
  15.2 12.9 %collective-permute-start = (bf16[16,5,128]{0,1,2:T(8,128)(2,1)}, bf16[16,5,128]{0,1,2:T(8,128)(2,1)S(1)}, u32[]{:S(2)}, u32[]{:S(2)}) collective-permute-start(bf16[16,5,128]{0,1,2:T(8,128)(2,1)} %get-tuple-element.158), channel_id=1, source_target_pairs={{0,4},{4,8},{8,12},{1,5},{5,9},{9,13},{2,6},{6,10},{10,14},{3,7},{... | collective-permute-start | bytes 61448 | tf_op jit(solution)/shard_map/ppermute | solution.py:13
  20.3 10.4 %collective-permute-start.1 = (bf16[16,5,128]{0,1,2:T(8,128)(2,1)S(1)}, bf16[16,5,128]{0,1,2:T(8,128)(2,1)S(1)}, u32[]{:S(2)}, u32[]{:S(2)}) collective-permute-start(bf16[16,5,128]{0,1,2:T(8,128)(2,1)S(1)} %get-tuple-element.160), channel_id=1, source_target_pairs={{4,0},{8,4},{12,8},{5,1},{9,5},{13,9},{6,2},{10,6},{14,10},{7,3},{... | collective-permute-start | bytes 61448 | tf_op jit(solution)/shard_map/ppermute | solution.py:13
  21.6 10.4 %collective-permute-start.2 = (bf16[16,5,128]{0,1,2:T(8,128)(2,1)}, bf16[16,5,128]{0,1,2:T(8,128)(2,1)S(1)}, u32[]{:S(2)}, u32[]{:S(2)}) collective-permute-start(bf16[16,5,128]{0,1,2:T(8,128)(2,1)} %get-tuple-element.157), channel_id=1, source_target_pairs={{0,4},{4,8},{8,12},{1,5},{5,9},{9,13},{2,6},{6,10},{10,14},{3,7},{... | collective-permute-start | bytes 61448 | tf_op jit(solution)/shard_map/ppermute | solution.py:13
  26.2 9.9 %collective-permute-start.3 = (bf16[16,5,128]{0,1,2:T(8,128)(2,1)S(1)}, bf16[16,5,128]{0,1,2:T(8,128)(2,1)S(1)}, u32[]{:S(2)}, u32[]{:S(2)}) collective-permute-start(bf16[16,5,128]{0,1,2:T(8,128)(2,1)S(1)} %get-tuple-element.159), channel_id=1, source_target_pairs={{4,0},{8,4},{12,8},{5,1},{9,5},{13,9},{6,2},{10,6},{14,10},{7,3},{... | collective-permute-start | bytes 61448 | tf_op jit(solution)/shard_map/ppermute | solution.py:13
  98.4 7.4 %copy-start.28 = (pred[512]{0:T(512)(128)(4,1)S(1)}, pred[512]{0:T(512)(128)(4,1)}, u32[]{:S(2)}) copy-start(pred[512]{0:T(512)(128)(4,1)} %compare_and_fusion.17) | copy-start | bytes 1540 | tf_op jit(solution)/shard_map/while
  105.8 7.4 %copy-start.27 = (pred[512]{0:T(512)(128)(4,1)S(1)}, pred[512]{0:T(512)(128)(4,1)}, u32[]{:S(2)}) copy-start(pred[512]{0:T(512)(128)(4,1)} %compare_and_fusion.16) | copy-start | bytes 1540 | tf_op jit(solution)/shard_map/while
  120.5 6.1 %copy-start.18 = (f32[1,512]{1,0:T(1,128)S(1)}, f32[1,512]{1,0:T(1,128)}, u32[]{:S(2)}) copy-start(f32[1,512]{1,0:T(1,128)} %get-tuple-element.261) | copy-start | bytes 6148 | tf_op jit(solution)/shard_map/while
  120.5 6.1 %copy-start.19 = (f32[1,512]{1,0:T(1,128)S(1)}, f32[1,512]{1,0:T(1,128)}, u32[]{:S(2)}) copy-start(f32[1,512]{1,0:T(1,128)} %get-tuple-element.251) | copy-start | bytes 6148 | tf_op jit(solution)/shard_map/while
  120.5 6.1 %copy-start.20 = (f32[1,512]{1,0:T(1,128)S(1)}, f32[1,512]{1,0:T(1,128)}, u32[]{:S(2)}) copy-start(f32[1,512]{1,0:T(1,128)} %get-tuple-element.253) | copy-start | bytes 6148 | tf_op jit(solution)/shard_map/while
  120.5 6.1 %copy-start.21 = (f32[1,512]{1,0:T(1,128)S(1)}, f32[1,512]{1,0:T(1,128)}, u32[]{:S(2)}) copy-start(f32[1,512]{1,0:T(1,128)} %get-tuple-element.255) | copy-start | bytes 6148 | tf_op jit(solution)/shard_map/while
  189.2 7.4 %copy-start.28 = (pred[512]{0:T(512)(128)(4,1)S(1)}, pred[512]{0:T(512)(128)(4,1)}, u32[]{:S(2)}) copy-start(pred[512]{0:T(512)(128)(4,1)} %compare_and_fusion.17) | copy-start | bytes 1540 | tf_op jit(solution)/shard_map/while
  196.6 7.4 %copy-start.27 = (pred[512]{0:T(512)(128)(4,1)S(1)}, pred[512]{0:T(512)(128)(4,1)}, u32[]{:S(2)}) copy-start(pred[512]{0:T(512)(128)(4,1)} %compare_and_fusion.16) | copy-start | bytes 1540 | tf_op jit(solution)/shard_map/while
  211.3 6.1 %copy-start.18 = (f32[1,512]{1,0:T(1,128)S(1)}, f32[1,512]{1,0:T(1,128)}, u32[]{:S(2)}) copy-start(f32[1,512]{1,0:T(1,128)} %get-tuple-element.261) | copy-start | bytes 6148 | tf_op jit(solution)/shard_map/while
  211.3 6.1 %copy-start.19 = (f32[1,512]{1,0:T(1,128)S(1)}, f32[1,512]{1,0:T(1,128)}, u32[]{:S(2)}) copy-start(f32[1,512]{1,0:T(1,128)} %get-tuple-element.251) | copy-start | bytes 6148 | tf_op jit(solution)/shard_map/while
  211.3 6.1 %copy-start.20 = (f32[1,512]{1,0:T(1,128)S(1)}, f32[1,512]{1,0:T(1,128)}, u32[]{:S(2)}) copy-start(f32[1,512]{1,0:T(1,128)} %get-tuple-element.253) | copy-start | bytes 6148 | tf_op jit(solution)/shard_map/while
  211.3 6.1 %copy-start.21 = (f32[1,512]{1,0:T(1,128)S(1)}, f32[1,512]{1,0:T(1,128)}, u32[]{:S(2)}) copy-start(f32[1,512]{1,0:T(1,128)} %get-tuple-element.255) | copy-start | bytes 6148 | tf_op jit(solution)/shard_map/while
  214.0 3.4 %copy-start.2 = (f32[8,5,768]{2,0,1:T(8,128)S(1)}, f32[8,5,768]{2,0,1:T(8,128)}, u32[]{:S(2)}) copy-start(f32[8,5,768]{2,0,1:T(8,128)} %copy-done.1) | copy-start | bytes 368644 | tf_op jit(solution)/shard_map/while
  214.0 3.4 %copy-start.6 = (f32[8,10,512]{2,0,1:T(8,128)S(1)}, f32[8,10,512]{2,0,1:T(8,128)}, u32[]{:S(2)}) copy-start(f32[8,10,512]{2,0,1:T(8,128)} %get-tuple-element.260) | copy-start | bytes 491524 | tf_op jit(solution)/shard_map/while
  214.0 3.4 %copy-start.7 = (f32[8,10,512]{2,0,1:T(8,128)S(1)}, f32[8,10,512]{2,0,1:T(8,128)}, u32[]{:S(2)}) copy-start(f32[8,10,512]{2,0,1:T(8,128)} %get-tuple-element.249) | copy-start | bytes 491524 | tf_op jit(solution)/shard_map/while
  214.1 3.4 %copy-start.8 = (f32[8,10,512]{2,0,1:T(8,128)S(1)}, f32[8,10,512]{2,0,1:T(8,128)}, u32[]{:S(2)}) copy-start(f32[8,10,512]{2,0,1:T(8,128)} %get-tuple-element.258) | copy-start | bytes 491524 | tf_op jit(solution)/shard_map/while
  214.1 3.4 %copy-start.9 = (f32[8,10,512]{2,0,1:T(8,128)S(1)}, f32[8,10,512]{2,0,1:T(8,128)}, u32[]{:S(2)}) copy-start(f32[8,10,512]{2,0,1:T(8,128)} %get-tuple-element.247) | copy-start | bytes 491524 | tf_op jit(solution)/shard_map/while
  214.1 3.4 %copy-start.10 = (f32[8,10,512]{2,0,1:T(8,128)S(1)}, f32[8,10,512]{2,0,1:T(8,128)}, u32[]{:S(2)}) copy-start(f32[8,10,512]{2,0,1:T(8,128)} %get-tuple-element.256) | copy-start | bytes 491524 | tf_op jit(solution)/shard_map/while
  214.1 3.4 %copy-start.11 = (f32[8,10,512]{2,0,1:T(8,128)S(1)}, f32[8,10,512]{2,0,1:T(8,128)}, u32[]{:S(2)}) copy-start(f32[8,10,512]{2,0,1:T(8,128)} %get-tuple-element.245) | copy-start | bytes 491524 | tf_op jit(solution)/shard_map/while
  214.1 3.4 %copy-start.12 = (f32[8,10,512]{2,0,1:T(8,128)S(1)}, f32[8,10,512]{2,0,1:T(8,128)}, u32[]{:S(2)}) copy-start(f32[8,10,512]{2,0,1:T(8,128)} %get-tuple-element.254) | copy-start | bytes 491524 | tf_op jit(solution)/shard_map/while
  214.1 3.4 %copy-start.13 = (f32[8,10,512]{2,0,1:T(8,128)S(1)}, f32[8,10,512]{2,0,1:T(8,128)}, u32[]{:S(2)}) copy-start(f32[8,10,512]{2,0,1:T(8,128)} %get-tuple-element.243) | copy-start | bytes 491524 | tf_op jit(solution)/shard_map/while
  214.1 3.4 %copy-start.22 = (f32[1,512]{1,0:T(1,128)S(1)}, f32[1,512]{1,0:T(1,128)}, u32[]{:S(2)}) copy-start(f32[1,512]{1,0:T(1,128)} %get-tuple-element.257) | copy-start | bytes 6148 | tf_op jit(solution)/shard_map/while
  214.1 3.4 %copy-start.23 = (f32[1,512]{1,0:T(1,128)S(1)}, f32[1,512]{1,0:T(1,128)}, u32[]{:S(2)}) copy-start(f32[1,512]{1,0:T(1,128)} %get-tuple-element.259) | copy-start | bytes 6148 | tf_op jit(solution)/shard_map/while
  214.1 3.4 %copy-start.24 = (bf16[2,8,5,512]{3,1,2,0:T(8,128)(2,1)S(1)}, bf16[2,8,5,512]{3,1,2,0:T(8,128)(2,1)}, u32[]{:S(2)}) copy-start(bf16[2,8,5,512]{3,1,2,0:T(8,128)(2,1)} %get-tuple-element.272) | copy-start | bytes 245764 | tf_op jit(solution)/shard_map/while
  (26 other events, 71.9 us)
where the time goes:
time: 232 us; the launch traced here: 230 us
  local copies, waits for them, and re-layouts  154 us (66%)
  other arithmetic  35.5 us (15%)
  blocking collectives  20.3 us (9%)
  starting transfers between devices  10.6 us (5%)
  waiting for transfers between devices  6.83 us (3%)
    gather x48, local copies, waits for them, and re-layouts, face_flux(): taken = jnp.take(stacked, neighbors[face_index], axis=2)  133 us
    select_n x24, other arithmetic, face_flux(): taken = jnp.take(stacked, neighbors[face_index], axis=2)  15.6 us
    psum x1, blocking collectives, local(): return lax.psum(closure_part, 'cell')  10.7 us
    ppermute x4, starting transfers between devices, from_behind(): return lax.ppermute(shard, axis, pairs)  10.6 us
    all_gather x1, blocking collectives, local(): whole_basis = lax.all_gather(basis, ('snap', 'var'), axis=0, tiled=True)  9.68 us
    concatenate x4, local copies, waits for them, and re-layouts, face_flux(): stacked = jnp.concatenate([extended, product], axis=1)  8.67 us
    ppermute x4, waiting for transfers between devices, from_behind(): return lax.ppermute(shard, axis, pairs)  6.83 us
    and x12, other arithmetic, face_flux(): taken = jnp.take(stacked, neighbors[face_index], axis=2)  6.67 us
  transfers between devices with their start and end apart: 4, of which 3 were waited for; matrix products, arithmetic and copies ran while one was open for 1% of the time, Pallas kernels for 0%

commit v1 on v0

--- a/solution.py
+++ b/solution.py
@@ -3,6 +3,7 @@
 import jax.numpy as jnp
 from jax import lax
 from jax.sharding import PartitionSpec as P
+from jax.lax import all_gather
 
 BLOCK = 128
 
@@ -69,7 +70,8 @@
     closure_part = lax.dot_general(
         weighted_flat, basis_flat, contract, preferred_element_type=jnp.float32
     )
-    return lax.psum(closure_part, "cell")
+    shape_the_set = lambda array_here: jnp.sum(all_gather(array_here, axis_name="cell"), 0)
+    return shape_the_set(closure_part)
 
 
 def solution(mesh):

time: 232 us -> 236 us (1.017)
  blocking collectives: 20.3 us -> 23 us
    all_gather x0 -> x1, blocking collectives: none -> 13.3 us  [local(): all_gather(array_here, axis_name='cell')]
    psum x1 -> x0, blocking collectives: 10.7 us -> none  [local(): return lax.psum(closure_part, 'cell')]
where the time goes in v1:
time: 236 us; the launch traced here: 234 us
  local copies, waits for them, and re-layouts  154 us (65%)
  other arithmetic  36.1 us (15%)
  blocking collectives  23 us (10%)
  starting transfers between devices  10.6 us (4%)
  waiting for transfers between devices  6.83 us (3%)
    gather x48, local copies, waits for them, and re-layouts, face_flux(): taken = jnp.take(stacked, neighbors[face_index], axis=2)  133 us
    select_n x24, other arithmetic, face_flux(): taken = jnp.take(stacked, neighbors[face_index], axis=2)  15.6 us
    all_gather x1, blocking collectives, local(): all_gather(array_here, axis_name='cell')  13.3 us
    ppermute x4, starting transfers between devices, from_behind(): return lax.ppermute(shard, axis, pairs)  10.6 us
    all_gather x1, blocking collectives, local(): whole_basis = lax.all_gather(basis, ('snap', 'var'), axis=0, tiled=True)  9.68 us
    concatenate x4, local copies, waits for them, and re-layouts, face_flux(): stacked = jnp.concatenate([extended, product], axis=1)  8.67 us
    ppermute x4, waiting for transfers between devices, from_behind(): return lax.ppermute(shard, axis, pairs)  6.83 us
    and x12, other arithmetic, face_flux(): taken = jnp.take(stacked, neighbors[face_index], axis=2)  6.67 us
  transfers between devices with their start and end apart: 4, of which 3 were waited for; matrix products, arithmetic and copies ran while one was open for 1% of the time, Pallas kernels for 0%

profile of v1, /device:TPU:0, one launch (start us, length us, event | category | flops | bytes accessed | tf_op | source)
XLA Modules:
  0.0 233.7 jit_solution(14607476594043309886)
XLA Ops:
  0.8 9.7 %all_gather.9 = bf16[128,5,512]{2,0,1:T(8,128)(2,1)S(1)} all-gather(bf16[32,5,512]{2,0,1:T(8,128)(2,1)} %param.16), channel_id=1, replica_groups=mesh['grp'=2,'cell'=4,'snap'=2,'var'=2] {'snap','var'}, dimensions={0}, use_global_device_ids=true | all-gather | bytes 819200 | tf_op jit(solution)/shard_map/all_gather | solution.py:43
  15.2 3.5 %collective-permute-start = (bf16[16,5,128]{0,1,2:T(8,128)(2,1)}, bf16[16,5,128]{0,1,2:T(8,128)(2,1)S(1)}, u32[]{:S(2)}, u32[]{:S(2)}) collective-permute-start(bf16[16,5,128]{0,1,2:T(8,128)(2,1)} %get-tuple-element.158), channel_id=1, source_target_pairs={{0,4},{4,8},{8,12},{1,5},{5,9},{9,13},{2,6},{6,10},{10,14},{3,7},{... | collective-permute-start | bytes 61448 | tf_op jit(solution)/shard_map/ppermute | solution.py:14
  21.6 4.6 %collective-permute-start.2 = (bf16[16,5,128]{0,1,2:T(8,128)(2,1)}, bf16[16,5,128]{0,1,2:T(8,128)(2,1)S(1)}, u32[]{:S(2)}, u32[]{:S(2)}) collective-permute-start(bf16[16,5,128]{0,1,2:T(8,128)(2,1)} %get-tuple-element.157), channel_id=1, source_target_pairs={{0,4},{4,8},{8,12},{1,5},{5,9},{9,13},{2,6},{6,10},{10,14},{3,7},{... | collective-permute-start | bytes 61448 | tf_op jit(solution)/shard_map/ppermute | solution.py:14
  32.1 4.0 %collective-permute-done.3 = bf16[16,5,128]{0,1,2:T(8,128)(2,1)S(1)} collective-permute-done((bf16[16,5,128]{0,1,2:T(8,128)(2,1)S(1)}, bf16[16,5,128]{0,1,2:T(8,128)(2,1)S(1)}, u32[]{:S(2)}, u32[]{:S(2)}) %collective-permute-start.3) | collective-permute-done | bytes 20512 | tf_op jit(solution)/shard_map/ppermute | solution.py:14
  36.9 181.6 %while.11 = (s32[]{:T(128)}, bf16[2,8,5,512]{3,1,2,0:T(8,128)(2,1)}, f32[5,512]{1,0:T(8,128)S(1)}, f32[6,512]{1,0:T(8,128)}, bf16[2,8,5,768]{3,1,0,2:T(8,128)(2,...) while((s32[]{:T(128)}, ...), condition=%wide.region_1.4_spmd.clone, body=%wide.region_0.3_spmd.clone.sunk | while | flops 2576898 | bytes 26133308 | solution.py:67
  49.7 2.8 %gather_fusion.11 = f32[512,8,10]{2,1,0:T(8,128)} fusion(f32[8,10,768]{1,0,2:T(8,128)S(1)} %copy.153, s32[1024]{0:T(1024)} %pad_clamp_fusion.19), kind=kCustom, calls=%fused_computation.10.clone.clone.1 | custom fusion | bytes 329728 | tf_op jit(solution)/shard_map/while/body/eval_jaxpr/jit(_take)/gather | solution.py:26
  52.5 2.9 %copy.164 = f32[512,8,10]{0,1,2:T(8,128)} copy(f32[512,8,10]{2,1,0:T(8,128)} %gather_fusion.11) | data formatting | bytes 327680 | tf_op jit(solution)/shard_map/while/body/eval_jaxpr/jit(_take)/gather | solution.py:26
  58.1 2.9 %copy.162 = f32[512,8,10]{0,1,2:T(8,128)} copy(f32[512,8,10]{2,1,0:T(8,128)} %gather_fusion.9) | data formatting | bytes 327680 | tf_op jit(solution)/shard_map/while/body/eval_jaxpr/jit(_take)/gather | solution.py:26
  63.6 2.9 %copy.160 = f32[512,8,10]{0,1,2:T(8,128)} copy(f32[512,8,10]{2,1,0:T(8,128)} %gather_fusion.7) | data formatting | bytes 327680 | tf_op jit(solution)/shard_map/while/body/eval_jaxpr/jit(_take)/gather | solution.py:26
  69.2 2.9 %copy.158 = f32[512,8,10]{0,1,2:T(8,128)} copy(f32[512,8,10]{2,1,0:T(8,128)} %gather_fusion.5) | data formatting | bytes 327680 | tf_op jit(solution)/shard_map/while/body/eval_jaxpr/jit(_take)/gather | solution.py:26
  74.8 2.9 %copy.156 = f32[512,8,10]{0,1,2:T(8,128)} copy(f32[512,8,10]{2,1,0:T(8,128)} %gather_fusion.3) | data formatting | bytes 327680 | tf_op jit(solution)/shard_map/while/body/eval_jaxpr/jit(_take)/gather | solution.py:26
  80.3 2.9 %copy.154 = f32[512,8,10]{0,1,2:T(8,128)} copy(f32[512,8,10]{2,1,0:T(8,128)} %gather_fusion.1) | data formatting | bytes 327680 | tf_op jit(solution)/shard_map/while/body/eval_jaxpr/jit(_take)/gather | solution.py:26
  85.4 2.8 %gather_fusion.10 = f32[512,8,10]{2,1,0:T(8,128)} fusion(f32[8,10,768]{1,0,2:T(8,128)S(1)} %copy.151, s32[1024]{0:T(1024)} %pad_clamp_fusion.19), kind=kCustom, calls=%fused_computation.1.clone.clone.1 | custom fusion | bytes 329728 | tf_op jit(solution)/shard_map/while/body/eval_jaxpr/jit(_take)/gather | solution.py:26
  88.2 2.9 %copy.163 = f32[512,8,10]{0,1,2:T(8,128)} copy(f32[512,8,10]{2,1,0:T(8,128)} %gather_fusion.10) | data formatting | bytes 327680 | tf_op jit(solution)/shard_map/while/body/eval_jaxpr/jit(_take)/gather | solution.py:26
  95.5 2.9 %copy.161 = f32[512,8,10]{0,1,2:T(8,128)} copy(f32[512,8,10]{2,1,0:T(8,128)} %gather_fusion.8) | data formatting | bytes 327680 | tf_op jit(solution)/shard_map/while/body/eval_jaxpr/jit(_take)/gather | solution.py:26
  102.9 2.9 %copy.159 = f32[512,8,10]{0,1,2:T(8,128)} copy(f32[512,8,10]{2,1,0:T(8,128)} %gather_fusion.6) | data formatting | bytes 327680 | tf_op jit(solution)/shard_map/while/body/eval_jaxpr/jit(_take)/gather | solution.py:26
  110.3 2.9 %copy.157 = f32[512,8,10]{0,1,2:T(8,128)} copy(f32[512,8,10]{2,1,0:T(8,128)} %gather_fusion.4) | data formatting | bytes 327680 | tf_op jit(solution)/shard_map/while/body/eval_jaxpr/jit(_take)/gather | solution.py:26
  117.6 2.9 %copy.155 = f32[512,8,10]{0,1,2:T(8,128)} copy(f32[512,8,10]{2,1,0:T(8,128)} %gather_fusion.2) | data formatting | bytes 327680 | tf_op jit(solution)/shard_map/while/body/eval_jaxpr/jit(_take)/gather | solution.py:26
  140.5 2.8 %gather_fusion.11 = f32[512,8,10]{2,1,0:T(8,128)} fusion(f32[8,10,768]{1,0,2:T(8,128)S(1)} %copy.153, s32[1024]{0:T(1024)} %pad_clamp_fusion.19), kind=kCustom, calls=%fused_computation.10.clone.clone.1 | custom fusion | bytes 329728 | tf_op jit(solution)/shard_map/while/body/eval_jaxpr/jit(_take)/gather | solution.py:26
  143.3 2.9 %copy.164 = f32[512,8,10]{0,1,2:T(8,128)} copy(f32[512,8,10]{2,1,0:T(8,128)} %gather_fusion.11) | data formatting | bytes 327680 | tf_op jit(solution)/shard_map/while/body/eval_jaxpr/jit(_take)/gather | solution.py:26
  148.9 2.9 %copy.162 = f32[512,8,10]{0,1,2:T(8,128)} copy(f32[512,8,10]{2,1,0:T(8,128)} %gather_fusion.9) | data formatting | bytes 327680 | tf_op jit(solution)/shard_map/while/body/eval_jaxpr/jit(_take)/gather | solution.py:26
  154.4 2.9 %copy.160 = f32[512,8,10]{0,1,2:T(8,128)} copy(f32[512,8,10]{2,1,0:T(8,128)} %gather_fusion.7) | data formatting | bytes 327680 | tf_op jit(solution)/shard_map/while/body/eval_jaxpr/jit(_take)/gather | solution.py:26
  160.0 2.9 %copy.158 = f32[512,8,10]{0,1,2:T(8,128)} copy(f32[512,8,10]{2,1,0:T(8,128)} %gather_fusion.5) | data formatting | bytes 327680 | tf_op jit(solution)/shard_map/while/body/eval_jaxpr/jit(_take)/gather | solution.py:26
  165.6 2.9 %copy.156 = f32[512,8,10]{0,1,2:T(8,128)} copy(f32[512,8,10]{2,1,0:T(8,128)} %gather_fusion.3) | data formatting | bytes 327680 | tf_op jit(solution)/shard_map/while/body/eval_jaxpr/jit(_take)/gather | solution.py:26
  171.1 2.9 %copy.154 = f32[512,8,10]{0,1,2:T(8,128)} copy(f32[512,8,10]{2,1,0:T(8,128)} %gather_fusion.1) | data formatting | bytes 327680 | tf_op jit(solution)/shard_map/while/body/eval_jaxpr/jit(_take)/gather | solution.py:26
  176.2 2.8 %gather_fusion.10 = f32[512,8,10]{2,1,0:T(8,128)} fusion(f32[8,10,768]{1,0,2:T(8,128)S(1)} %copy.151, s32[1024]{0:T(1024)} %pad_clamp_fusion.19), kind=kCustom, calls=%fused_computation.1.clone.clone.1 | custom fusion | bytes 329728 | tf_op jit(solution)/shard_map/while/body/eval_jaxpr/jit(_take)/gather | solution.py:26
  179.0 2.9 %copy.163 = f32[512,8,10]{0,1,2:T(8,128)} copy(f32[512,8,10]{2,1,0:T(8,128)} %gather_fusion.10) | data formatting | bytes 327680 | tf_op jit(solution)/shard_map/while/body/eval_jaxpr/jit(_take)/gather | solution.py:26
  186.3 2.9 %copy.161 = f32[512,8,10]{0,1,2:T(8,128)} copy(f32[512,8,10]{2,1,0:T(8,128)} %gather_fusion.8) | data formatting | bytes 327680 | tf_op jit(solution)/shard_map/while/body/eval_jaxpr/jit(_take)/gather | solution.py:26
  193.7 2.9 %copy.159 = f32[512,8,10]{0,1,2:T(8,128)} copy(f32[512,8,10]{2,1,0:T(8,128)} %gather_fusion.6) | data formatting | bytes 327680 | tf_op jit(solution)/shard_map/while/body/eval_jaxpr/jit(_take)/gather | solution.py:26
  201.1 2.9 %copy.157 = f32[512,8,10]{0,1,2:T(8,128)} copy(f32[512,8,10]{2,1,0:T(8,128)} %gather_fusion.4) | data formatting | bytes 327680 | tf_op jit(solution)/shard_map/while/body/eval_jaxpr/jit(_take)/gather | solution.py:26
  208.4 2.9 %copy.155 = f32[512,8,10]{0,1,2:T(8,128)} copy(f32[512,8,10]{2,1,0:T(8,128)} %gather_fusion.2) | data formatting | bytes 327680 | tf_op jit(solution)/shard_map/while/body/eval_jaxpr/jit(_take)/gather | solution.py:26
  219.8 13.3 %all-gather = f32[64,128]{1,0:T(8,128)S(1)} all-gather(f32[16,128]{1,0:T(8,128)S(1)} %fusion.66), channel_id=2, replica_groups=mesh['grp'=2,'cell'=4,'snap'=2,'var'=2] {'cell'}, dimensions={0}, use_global_device_ids=true | all-gather | bytes 40960 | tf_op jit(solution)/shard_map/all_gather | solution.py:73
  (234 shorter events, 122.4 us)
Async XLA Ops:
  0.0 10.8 %copy-start = (bf16[16,128]{1,0:T(8,128)(2,1)S(1)}, bf16[16,128]{1,0:T(8,128)(2,1)}, u32[]{:S(2)}) copy-start(bf16[16,128]{1,0:T(8,128)(2,1)} %param.15) | copy-start | bytes 12292
  0.8 11.3 %copy-start.17 = (bf16[16,5,512]{2,0,1:T(8,128)(2,1)S(1)}, bf16[16,5,512]{2,0,1:T(8,128)(2,1)}, u32[]{:S(2)}) copy-start(bf16[16,5,512]{2,0,1:T(8,128)(2,1)} %param.14) | copy-start | bytes 245764
  10.8 4.4 %copy-start.14 = (bf16[128,5,512]{0,2,1:T(8,128)(2,1)}, bf16[128,5,512]{0,2,1:T(8,128)(2,1)S(1)}, u32[]{:S(2)}) copy-start(bf16[128,5,512]{0,2,1:T(8,128)(2,1)S(1)} %copy.124) | copy-start | bytes 1966084
  12.8 24.1 %copy-start.15 = (f32[5,512]{1,0:T(8,128)S(1)}, f32[5,512]{1,0:T(8,128)}, u32[]{:S(2)}) copy-start(f32[5,512]{1,0:T(8,128)} %param.17) | copy-start | bytes 30724
  15.2 12.9 %collective-permute-start = (bf16[16,5,128]{0,1,2:T(8,128)(2,1)}, bf16[16,5,128]{0,1,2:T(8,128)(2,1)S(1)}, u32[]{:S(2)}, u32[]{:S(2)}) collective-permute-start(bf16[16,5,128]{0,1,2:T(8,128)(2,1)} %get-tuple-element.158), channel_id=1, source_target_pairs={{0,4},{4,8},{8,12},{1,5},{5,9},{9,13},{2,6},{6,10},{10,14},{3,7},{... | collective-permute-start | bytes 61448 | tf_op jit(solution)/shard_map/ppermute | solution.py:14
  20.3 10.4 %collective-permute-start.1 = (bf16[16,5,128]{0,1,2:T(8,128)(2,1)S(1)}, bf16[16,5,128]{0,1,2:T(8,128)(2,1)S(1)}, u32[]{:S(2)}, u32[]{:S(2)}) collective-permute-start(bf16[16,5,128]{0,1,2:T(8,128)(2,1)S(1)} %get-tuple-element.160), channel_id=1, source_target_pairs={{4,0},{8,4},{12,8},{5,1},{9,5},{13,9},{6,2},{10,6},{14,10},{7,3},{... | collective-permute-start | bytes 61448 | tf_op jit(solution)/shard_map/ppermute | solution.py:14
  21.6 10.4 %collective-permute-start.2 = (bf16[16,5,128]{0,1,2:T(8,128)(2,1)}, bf16[16,5,128]{0,1,2:T(8,128)(2,1)S(1)}, u32[]{:S(2)}, u32[]{:S(2)}) collective-permute-start(bf16[16,5,128]{0,1,2:T(8,128)(2,1)} %get-tuple-element.157), channel_id=1, source_target_pairs={{0,4},{4,8},{8,12},{1,5},{5,9},{9,13},{2,6},{6,10},{10,14},{3,7},{... | collective-permute-start | bytes 61448 | tf_op jit(solution)/shard_map/ppermute | solution.py:14
  26.2 9.9 %collective-permute-start.3 = (bf16[16,5,128]{0,1,2:T(8,128)(2,1)S(1)}, bf16[16,5,128]{0,1,2:T(8,128)(2,1)S(1)}, u32[]{:S(2)}, u32[]{:S(2)}) collective-permute-start(bf16[16,5,128]{0,1,2:T(8,128)(2,1)S(1)} %get-tuple-element.159), channel_id=1, source_target_pairs={{4,0},{8,4},{12,8},{5,1},{9,5},{13,9},{6,2},{10,6},{14,10},{7,3},{... | collective-permute-start | bytes 61448 | tf_op jit(solution)/shard_map/ppermute | solution.py:14
  98.4 7.4 %copy-start.28 = (pred[512]{0:T(512)(128)(4,1)S(1)}, pred[512]{0:T(512)(128)(4,1)}, u32[]{:S(2)}) copy-start(pred[512]{0:T(512)(128)(4,1)} %compare_and_fusion.17) | copy-start | bytes 1540 | tf_op jit(solution)/shard_map/while
  105.8 7.4 %copy-start.27 = (pred[512]{0:T(512)(128)(4,1)S(1)}, pred[512]{0:T(512)(128)(4,1)}, u32[]{:S(2)}) copy-start(pred[512]{0:T(512)(128)(4,1)} %compare_and_fusion.16) | copy-start | bytes 1540 | tf_op jit(solution)/shard_map/while
  120.5 6.1 %copy-start.18 = (f32[1,512]{1,0:T(1,128)S(1)}, f32[1,512]{1,0:T(1,128)}, u32[]{:S(2)}) copy-start(f32[1,512]{1,0:T(1,128)} %get-tuple-element.261) | copy-start | bytes 6148 | tf_op jit(solution)/shard_map/while
  120.5 6.1 %copy-start.19 = (f32[1,512]{1,0:T(1,128)S(1)}, f32[1,512]{1,0:T(1,128)}, u32[]{:S(2)}) copy-start(f32[1,512]{1,0:T(1,128)} %get-tuple-element.251) | copy-start | bytes 6148 | tf_op jit(solution)/shard_map/while
  120.5 6.1 %copy-start.20 = (f32[1,512]{1,0:T(1,128)S(1)}, f32[1,512]{1,0:T(1,128)}, u32[]{:S(2)}) copy-start(f32[1,512]{1,0:T(1,128)} %get-tuple-element.253) | copy-start | bytes 6148 | tf_op jit(solution)/shard_map/while
  120.5 6.1 %copy-start.21 = (f32[1,512]{1,0:T(1,128)S(1)}, f32[1,512]{1,0:T(1,128)}, u32[]{:S(2)}) copy-start(f32[1,512]{1,0:T(1,128)} %get-tuple-element.255) | copy-start | bytes 6148 | tf_op jit(solution)/shard_map/while
  189.2 7.4 %copy-start.28 = (pred[512]{0:T(512)(128)(4,1)S(1)}, pred[512]{0:T(512)(128)(4,1)}, u32[]{:S(2)}) copy-start(pred[512]{0:T(512)(128)(4,1)} %compare_and_fusion.17) | copy-start | bytes 1540 | tf_op jit(solution)/shard_map/while
  196.6 7.4 %copy-start.27 = (pred[512]{0:T(512)(128)(4,1)S(1)}, pred[512]{0:T(512)(128)(4,1)}, u32[]{:S(2)}) copy-start(pred[512]{0:T(512)(128)(4,1)} %compare_and_fusion.16) | copy-start | bytes 1540 | tf_op jit(solution)/shard_map/while
  211.3 6.1 %copy-start.18 = (f32[1,512]{1,0:T(1,128)S(1)}, f32[1,512]{1,0:T(1,128)}, u32[]{:S(2)}) copy-start(f32[1,512]{1,0:T(1,128)} %get-tuple-element.261) | copy-start | bytes 6148 | tf_op jit(solution)/shard_map/while
  211.3 6.1 %copy-start.19 = (f32[1,512]{1,0:T(1,128)S(1)}, f32[1,512]{1,0:T(1,128)}, u32[]{:S(2)}) copy-start(f32[1,512]{1,0:T(1,128)} %get-tuple-element.251) | copy-start | bytes 6148 | tf_op jit(solution)/shard_map/while
  211.3 6.1 %copy-start.20 = (f32[1,512]{1,0:T(1,128)S(1)}, f32[1,512]{1,0:T(1,128)}, u32[]{:S(2)}) copy-start(f32[1,512]{1,0:T(1,128)} %get-tuple-element.253) | copy-start | bytes 6148 | tf_op jit(solution)/shard_map/while
  211.3 6.1 %copy-start.21 = (f32[1,512]{1,0:T(1,128)S(1)}, f32[1,512]{1,0:T(1,128)}, u32[]{:S(2)}) copy-start(f32[1,512]{1,0:T(1,128)} %get-tuple-element.255) | copy-start | bytes 6148 | tf_op jit(solution)/shard_map/while
  214.0 3.4 %copy-start.2 = (f32[8,5,768]{2,0,1:T(8,128)S(1)}, f32[8,5,768]{2,0,1:T(8,128)}, u32[]{:S(2)}) copy-start(f32[8,5,768]{2,0,1:T(8,128)} %copy-done.1) | copy-start | bytes 368644 | tf_op jit(solution)/shard_map/while
  214.0 3.4 %copy-start.6 = (f32[8,10,512]{2,0,1:T(8,128)S(1)}, f32[8,10,512]{2,0,1:T(8,128)}, u32[]{:S(2)}) copy-start(f32[8,10,512]{2,0,1:T(8,128)} %get-tuple-element.260) | copy-start | bytes 491524 | tf_op jit(solution)/shard_map/while
  214.0 3.4 %copy-start.7 = (f32[8,10,512]{2,0,1:T(8,128)S(1)}, f32[8,10,512]{2,0,1:T(8,128)}, u32[]{:S(2)}) copy-start(f32[8,10,512]{2,0,1:T(8,128)} %get-tuple-element.249) | copy-start | bytes 491524 | tf_op jit(solution)/shard_map/while
  214.1 3.4 %copy-start.8 = (f32[8,10,512]{2,0,1:T(8,128)S(1)}, f32[8,10,512]{2,0,1:T(8,128)}, u32[]{:S(2)}) copy-start(f32[8,10,512]{2,0,1:T(8,128)} %get-tuple-element.258) | copy-start | bytes 491524 | tf_op jit(solution)/shard_map/while
  214.1 3.4 %copy-start.9 = (f32[8,10,512]{2,0,1:T(8,128)S(1)}, f32[8,10,512]{2,0,1:T(8,128)}, u32[]{:S(2)}) copy-start(f32[8,10,512]{2,0,1:T(8,128)} %get-tuple-element.247) | copy-start | bytes 491524 | tf_op jit(solution)/shard_map/while
  214.1 3.4 %copy-start.10 = (f32[8,10,512]{2,0,1:T(8,128)S(1)}, f32[8,10,512]{2,0,1:T(8,128)}, u32[]{:S(2)}) copy-start(f32[8,10,512]{2,0,1:T(8,128)} %get-tuple-element.256) | copy-start | bytes 491524 | tf_op jit(solution)/shard_map/while
  214.1 3.4 %copy-start.11 = (f32[8,10,512]{2,0,1:T(8,128)S(1)}, f32[8,10,512]{2,0,1:T(8,128)}, u32[]{:S(2)}) copy-start(f32[8,10,512]{2,0,1:T(8,128)} %get-tuple-element.245) | copy-start | bytes 491524 | tf_op jit(solution)/shard_map/while
  214.1 3.4 %copy-start.12 = (f32[8,10,512]{2,0,1:T(8,128)S(1)}, f32[8,10,512]{2,0,1:T(8,128)}, u32[]{:S(2)}) copy-start(f32[8,10,512]{2,0,1:T(8,128)} %get-tuple-element.254) | copy-start | bytes 491524 | tf_op jit(solution)/shard_map/while
  214.1 3.4 %copy-start.13 = (f32[8,10,512]{2,0,1:T(8,128)S(1)}, f32[8,10,512]{2,0,1:T(8,128)}, u32[]{:S(2)}) copy-start(f32[8,10,512]{2,0,1:T(8,128)} %get-tuple-element.243) | copy-start | bytes 491524 | tf_op jit(solution)/shard_map/while
  214.1 3.4 %copy-start.22 = (f32[1,512]{1,0:T(1,128)S(1)}, f32[1,512]{1,0:T(1,128)}, u32[]{:S(2)}) copy-start(f32[1,512]{1,0:T(1,128)} %get-tuple-element.257) | copy-start | bytes 6148 | tf_op jit(solution)/shard_map/while
  214.1 3.4 %copy-start.23 = (f32[1,512]{1,0:T(1,128)S(1)}, f32[1,512]{1,0:T(1,128)}, u32[]{:S(2)}) copy-start(f32[1,512]{1,0:T(1,128)} %get-tuple-element.259) | copy-start | bytes 6148 | tf_op jit(solution)/shard_map/while
  214.1 3.4 %copy-start.24 = (bf16[2,8,5,512]{3,1,2,0:T(8,128)(2,1)S(1)}, bf16[2,8,5,512]{3,1,2,0:T(8,128)(2,1)}, u32[]{:S(2)}) copy-start(bf16[2,8,5,512]{3,1,2,0:T(8,128)(2,1)} %get-tuple-element.272) | copy-start | bytes 245764 | tf_op jit(solution)/shard_map/while
  (26 other events, 71.9 us)
